TPU v7x, 32 devices: a whole 2x2x4 slice. The times are simulated.
32 devices in a mesh: pair: 2 (over x), blk: 8 (over z, y), group: 2 (over core).
Axes of the slice: x: 2, y: 2, z: 4, core: 2. Of those that a mesh axis runs over, the one named last changes fastest.
Arguments:
- codes: int32 [32, 1536, 256], P(('pair', 'blk', 'group')), may hold values from 0 to 255
- scales: int32 [32, 1536, 8], P(('pair', 'blk', 'group')), may hold values from -7 to 0
- inputs: bfloat16 [4096, 1536], P(('pair', 'blk', 'group')), may hold values from -6 to 6
- cotangent: bfloat16 [4096, 256], P(('pair', 'blk', 'group')), may hold values from -6 to 6
Outputs:
- earlier_grad: float32 [1536, 256], replicated
- current_grad: float32 [1536, 256], replicated
All inputs are finite; a program needn't handle non-finite values.
Results may differ from a plain program's by a relative error of at most 0.0003.
Values sent between devices are 32-bit elements; how exact they have to be, the bound alone decides.
No kernel may reach another device: no remote copies, remote signals or barrier semaphores. Data moves between devices by JAX's collectives and lax.ppermute only.
A program may use at most 64 MiB of HBM per device.

v0:
```python
import jax
import jax.numpy as jnp
from jax import lax
from jax.sharding import PartitionSpec as P


def decode(codes, scales):
    codes = codes[0]
    scales = scales[0]
    rows, width = codes.shape
    sign = 1.0 - 2.0 * (codes // 128).astype(jnp.float32)
    field = codes // 8 % 16
    mant = (codes % 8).astype(jnp.float32)
    frac = jnp.where(field > 0, 8.0 + mant, mant)
    power = jnp.where(field > 0, field, 1) - 10
    expo = power.reshape(rows, scales.shape[1], width // scales.shape[1]) + scales[:, :, None]
    return sign * frac * jnp.exp2(expo.reshape(rows, width).astype(jnp.float32))


def combine(stack, count):
    pooled = lax.psum(stack, "pair")
    share = lax.psum_scatter(pooled, "blk", scatter_dimension=1, tiled=True)
    total = lax.psum_scatter(share, "group", scatter_dimension=1, tiled=True) / count
    return lax.all_gather(total, ("blk", "group"), axis=1, tiled=True)


def key_product(inputs, cotangent):
    return lax.dot_general(
        inputs, cotangent, (((0,), (0,)), ((), ())), preferred_element_type=jnp.float32
    )


def local(codes, scales, inputs, cotangent):
    count = lax.axis_size("pair") * lax.axis_size("blk") * lax.axis_size("group")
    decoded = decode(codes, scales)
    product = key_product(inputs, cotangent)
    summed = combine(jnp.stack([decoded, product]), count)
    earlier_grad = summed[0]
    current_grad = summed[1]
    return (earlier_grad, current_grad)


def solution(mesh):
    in_specs = (
        P(("pair", "blk", "group"), None, None),
        P(("pair", "blk", "group"), None, None),
        P(("pair", "blk", "group"), None),
        P(("pair", "blk", "group"), None),
    )
    out_specs = (P(), P())
    return jax.shard_map(local, mesh=mesh, in_specs=in_specs, out_specs=out_specs, check_vma=False)
```

profile of v0, /device:TPU:0, one launch (start us, length us, event | category | flops | bytes accessed | tf_op | source)
XLA Modules:
  0.0 186.2 jit_solution(1373778970033017761)
XLA Ops:
  7.2 0.0 copy-start
  7.2 0.0 reduce-scatter.3.cloned.1.call-start
  7.2 1.0 add.58
  8.2 0.5 copy.7
  8.7 0.0 copy-start.1
  8.7 4.5 %fusion.5 = f32[1,1536,256]{2,1,0:T(8,128)S(1)} fusion(s32[1,1536,256]{2,1,0:T(8,128)S(1)} %copy.7, s32[1,1536,256]{2,1,0:T(8,128)} %param.4), kind=kLoop, calls=%fused_computation.20 | loop fusion | flops 21233664 | bytes 4718592 | tf_op jit(solution)/shard_map/mul | solution.py:17
  13.2 0.0 copy-done
  13.2 0.0 copy-done.1
  13.3 0.4 convolution_bitcast_fusion
  13.6 1.9 pad_maximum_fusion
  15.5 0.0 reduce-scatter.3.cloned.1.call-update
  15.5 0.0 reduce-scatter.5.cloned.1.call-start
  15.6 77.1 %reduce-scatter.3.cloned.1.call-done = f32[2,192,256]{2,1,0:T(8,128)} async-done(((f32[2,1536,256]{2,1,0:T(8,128)}), f32[2,192,256]{2,1,0:T(8,128)}) %reduce-scatter.3.cloned.1.call-update) | async-done | bytes 393232 | tf_op jit(solution)/shard_map/reduce_scatter | solution.py:22
  92.7 0.0 reduce-scatter.5.cloned.1.call-update
  92.7 0.0 all-reduce.2.cloned.1.call-start
  92.8 9.1 %reduce-scatter.5.cloned.1.call-done = f32[2,96,256]{2,1,0:T(8,128)} async-done(((f32[2,192,256]{2,1,0:T(8,128)}), f32[2,96,256]{2,1,0:T(8,128)}) %reduce-scatter.5.cloned.1.call-update) | async-done | bytes 196624 | tf_op jit(solution)/shard_map/reduce_scatter | solution.py:23
  101.9 0.0 all-reduce.2.cloned.1.call-update
  101.9 0.0 all-gather.2.cloned.1.call-start
  102.0 25.8 %all-reduce.2.cloned.1.call-done = f32[2,96,256]{2,1,0:T(8,128)} async-done(((f32[2,96,256]{2,1,0:T(8,128)}), f32[2,96,256]{2,1,0:T(8,128)}) %all-reduce.2.cloned.1.call-update) | async-done | bytes 196624 | tf_op jit(solution)/shard_map/psum | solution.py:21
  127.7 1.6 broadcast_multiply_fusion
  129.3 0.0 all-gather.2.cloned.1.call-update
  129.4 46.6 %all-gather.2.cloned.1.call-done = f32[2,1536,256]{2,1,0:T(8,128)} async-done(((f32[2,96,256]{2,1,0:T(8,128)}), f32[2,1536,256]{2,1,0:T(8,128)}) %all-gather.2.cloned.1.call-update) | async-done | bytes 3145744 | tf_op jit(solution)/shard_map/all_gather | solution.py:24
  176.0 3.7 %slice_bitcast_fusion = (f32[1536,256]{1,0:T(8,128)}, f32[1536,256]{1,0:T(8,128)}) fusion(f32[2,1536,256]{2,1,0:T(8,128)} %all-gather.2.cloned.1.call-done), kind=kLoop, calls=%fused_computation.28 | loop fusion | bytes 6291456 | tf_op jit(solution)/shard_map/squeeze | solution.py:39
Async XLA Ops:
  7.2 6.1 %copy-start = (bf16[128,1536]{1,0:T(8,128)(2,1)S(1)}, bf16[128,1536]{1,0:T(8,128)(2,1)}, u32[]{:S(2)}) copy-start(bf16[128,1536]{1,0:T(8,128)(2,1)} %param.6) | copy-start | bytes 1179652
  7.2 85.5 %reduce-scatter.3.cloned.1.call-start = ((), (), s32[]{:S(2)}) async-start(), calls=%async_computation.3 | async-start | bytes 3538944 | tf_op jit(solution)/shard_map/reduce_scatter | solution.py:22
  8.7 4.5 %copy-start.1 = (bf16[128,256]{1,0:T(8,128)(2,1)S(1)}, bf16[128,256]{1,0:T(8,128)(2,1)}, u32[]{:S(2)}) copy-start(bf16[128,256]{1,0:T(8,128)(2,1)} %param.7) | copy-start | bytes 196612
  15.5 86.4 %reduce-scatter.5.cloned.1.call-start = ((), (), s32[]{:S(2)}) async-start(), calls=%async_computation.4 | async-start | bytes 589824 | tf_op jit(solution)/shard_map/reduce_scatter | solution.py:23
  92.7 35.0 %all-reduce.2.cloned.1.call-start = ((), (), s32[]{:S(2)}) async-start(), calls=%async_computation.5 | async-start | bytes 393216 | tf_op jit(solution)/shard_map/psum | solution.py:21
  101.9 74.0 %all-gather.2.cloned.1.call-start = ((), (), s32[]{:S(2)}) async-start(), calls=%async_computation.2 | async-start | bytes 3342336 | tf_op jit(solution)/shard_map/all_gather | solution.py:24
Sparse Core Ops, SparseCore 0:
  15.7 77.0 reduce-scatter.2
  94.9 6.8 reduce-scatter.4
  104.2 23.5 all-reduce.1
  130.4 45.4 all-gather.1
where the time goes:
time: 186 us
  waiting for transfers between devices  159 us (85%)
  between operations  13.8 us (7%)
  other arithmetic  7.97 us (4%)
  local copies, waits for them, and re-layouts  5.23 us (3%)
    reduce_scatter x1, waiting for transfers between devices, combine(): share = lax.psum_scatter(pooled, 'blk', scatter_dimension=1, tiled=True)  77.1 us
    all_gather x1, waiting for transfers between devices, combine(): return lax.all_gather(total, ('blk', 'group'), axis=1, tiled=True)  46.6 us
    psum x1, waiting for transfers between devices, combine(): pooled = lax.psum(stack, 'pair')  25.8 us
    reduce_scatter x1, waiting for transfers between devices, combine(): lax.psum_scatter(share, 'group', scatter_dimension=1, tiled=True) / count  9.11 us
    mul x1, other arithmetic, decode(): return sign * frac * jnp.exp2(expo.reshape(rows, width).astype(jnp.float32))  4.5 us
    squeeze x1, local copies, waits for them, and re-layouts, local(): current_grad = summed[1]  3.74 us
  transfers between devices with their start and end apart: 4, of which 4 were waited for; matrix products, arithmetic and copies ran while one was open for 0% of the time, Pallas kernels for 0%

commit v1 on v0

--- a/solution.py
+++ b/solution.py
@@ -1,7 +1,17 @@
+import functools
 import jax
 import jax.numpy as jnp
 from jax import lax
 from jax.sharding import PartitionSpec as P
+from jax.lax import all_gather
+
+
+def manage_goods(matrix, chip_axis):
+    after = all_gather(matrix, chip_axis).sum(axis=0)
+    return after
+
+
+do_the_points = functools.partial(manage_goods, chip_axis="pair")
 
 
 def decode(codes, scales):
@@ -18,7 +28,7 @@
 
 
 def combine(stack, count):
-    pooled = lax.psum(stack, "pair")
+    pooled = do_the_points(stack)
     share = lax.psum_scatter(pooled, "blk", scatter_dimension=1, tiled=True)
     total = lax.psum_scatter(share, "group", scatter_dimension=1, tiled=True) / count
     return lax.all_gather(total, ("blk", "group"), axis=1, tiled=True)

time: 186 us -> 248 us (1.33)
  waiting for transfers between devices: 159 us -> 214 us
  other arithmetic: 7.97 us -> 13.3 us
    all_gather x0 -> x1, waiting for transfers between devices: none -> 83.2 us  [manage_goods(): after = all_gather(matrix, chip_axis).sum(axis=0)]
    psum x1 -> x0, waiting for transfers between devices: 25.8 us -> none  [combine(): pooled = lax.psum(stack, 'pair')]
    reduce_sum x0 -> x1, other arithmetic: none -> 5.3 us  [manage_goods(): after = all_gather(matrix, chip_axis).sum(axis=0)]
    reduce_scatter x1, waiting for transfers between devices: 77.1 us -> 74.4 us  [combine(): share = lax.psum_scatter(pooled, 'blk', scatter_dimension=1, tiled=True)]
where the time goes in v1:
time: 248 us; the launch traced here: 247 us
  waiting for transfers between devices  214 us (86%)
  between operations  13.8 us (6%)
  other arithmetic  13.3 us (5%)
  local copies, waits for them, and re-layouts  5.23 us (2%)
    all_gather x1, waiting for transfers between devices, manage_goods(): after = all_gather(matrix, chip_axis).sum(axis=0)  83.2 us
    reduce_scatter x1, waiting for transfers between devices, combine(): share = lax.psum_scatter(pooled, 'blk', scatter_dimension=1, tiled=True)  74.4 us
    all_gather x1, waiting for transfers between devices, combine(): return lax.all_gather(total, ('blk', 'group'), axis=1, tiled=True)  47.7 us
    reduce_scatter x1, waiting for transfers between devices, combine(): lax.psum_scatter(share, 'group', scatter_dimension=1, tiled=True) / count  9.12 us
    reduce_sum x1, other arithmetic, manage_goods(): after = all_gather(matrix, chip_axis).sum(axis=0)  5.3 us
  transfers between devices with their start and end apart: 4, of which 4 were waited for; matrix products, arithmetic and copies ran while one was open for 0% of the time, Pallas kernels for 0%

profile of v1, /device:TPU:0, one launch (start us, length us, event | category | flops | bytes accessed | tf_op | source)
XLA Modules:
  0.0 247.4 jit_solution(6054982789926673420)
XLA Ops:
  7.2 0.0 copy-start
  7.2 0.0 all-gather.6.cloned.1.call-start
  7.2 1.0 add.56
  8.2 0.5 copy.8
  8.7 0.0 copy-start.1
  8.7 4.5 %fusion.5 = f32[1,1536,256]{2,1,0:T(8,128)S(1)} fusion(s32[1,1536,256]{2,1,0:T(8,128)S(1)} %copy.8, s32[1,1536,256]{2,1,0:T(8,128)} %param.4), kind=kLoop, calls=%fused_computation.20 | loop fusion | flops 21233664 | bytes 4718592 | tf_op jit(solution)/shard_map/mul | solution.py:27
  13.2 0.0 copy-done
  13.2 0.0 copy-done.1
  13.3 0.4 convolution_bitcast_fusion
  13.6 1.9 pad_maximum_fusion
  15.6 0.0 all-gather.6.cloned.1.call-update
  15.6 0.0 reduce-scatter.3.cloned.1.call-start
  15.6 83.2 %all-gather.6.cloned.1.call-done = f32[4,1536,256]{2,1,0:T(8,128)} async-done(((f32[2,1536,256]{2,1,0:T(8,128)}), f32[4,1536,256]{2,1,0:T(8,128)}) %all-gather.6.cloned.1.call-update) | async-done | bytes 6291472 | tf_op jit(solution)/shard_map/all_gather | solution.py:10
  98.8 5.3 %reduce_sum.9 = f32[2,1536,256]{2,1,0:T(8,128)} reduce(f32[2,2,1536,256]{3,2,1,0:T(8,128)} %bitcast.11, f32[]{:T(128)} %constant.65.clone.1), dimensions={0}, to_apply=%region_0.1 | reduce | flops 786432 | bytes 9437188 | tf_op jit(solution)/shard_map/reduce_sum | solution.py:10
  104.1 0.0 reduce-scatter.3.cloned.1.call-update
  104.1 0.0 reduce-scatter.5.cloned.1.call-start
  104.2 74.4 %reduce-scatter.3.cloned.1.call-done = f32[2,192,256]{2,1,0:T(8,128)} async-done(((f32[2,1536,256]{2,1,0:T(8,128)}), f32[2,192,256]{2,1,0:T(8,128)}) %reduce-scatter.3.cloned.1.call-update) | async-done | bytes 393232 | tf_op jit(solution)/shard_map/reduce_scatter | solution.py:32
  178.6 0.0 reduce-scatter.5.cloned.1.call-update
  178.6 0.0 all-gather.4.cloned.1.call-start
  178.7 9.1 %reduce-scatter.5.cloned.1.call-done = f32[2,96,256]{2,1,0:T(8,128)} async-done(((f32[2,192,256]{2,1,0:T(8,128)}), f32[2,96,256]{2,1,0:T(8,128)}) %reduce-scatter.5.cloned.1.call-update) | async-done | bytes 196624 | tf_op jit(solution)/shard_map/reduce_scatter | solution.py:33
  187.8 1.6 broadcast_multiply_fusion
  189.4 0.0 all-gather.4.cloned.1.call-update
  189.4 47.7 %all-gather.4.cloned.1.call-done = f32[2,1536,256]{2,1,0:T(8,128)} async-done(((f32[2,96,256]{2,1,0:T(8,128)}), f32[2,1536,256]{2,1,0:T(8,128)}) %all-gather.4.cloned.1.call-update) | async-done | bytes 3145744 | tf_op jit(solution)/shard_map/all_gather | solution.py:34
  237.1 3.7 %slice_bitcast_fusion = (f32[1536,256]{1,0:T(8,128)}, f32[1536,256]{1,0:T(8,128)}) fusion(f32[2,1536,256]{2,1,0:T(8,128)} %all-gather.4.cloned.1.call-done), kind=kLoop, calls=%fused_computation.28 | loop fusion | bytes 6291456 | tf_op jit(solution)/shard_map/squeeze | solution.py:49
Async XLA Ops:
  7.2 6.1 %copy-start = (bf16[128,1536]{1,0:T(8,128)(2,1)S(1)}, bf16[128,1536]{1,0:T(8,128)(2,1)}, u32[]{:S(2)}) copy-start(bf16[128,1536]{1,0:T(8,128)(2,1)} %param.6) | copy-start | bytes 1179652
  7.2 91.6 %all-gather.6.cloned.1.call-start = ((), (), s32[]{:S(2)}) async-start(), calls=%async_computation.5 | async-start | bytes 9437184 | tf_op jit(solution)/shard_map/all_gather | solution.py:10
  8.7 4.5 %copy-start.1 = (bf16[128,256]{1,0:T(8,128)(2,1)S(1)}, bf16[128,256]{1,0:T(8,128)(2,1)}, u32[]{:S(2)}) copy-start(bf16[128,256]{1,0:T(8,128)(2,1)} %param.7) | copy-start | bytes 196612
  15.6 163.0 %reduce-scatter.3.cloned.1.call-start = ((), (), s32[]{:S(2)}) async-start(), calls=%async_computation.2 | async-start | bytes 3538944 | tf_op jit(solution)/shard_map/reduce_scatter | solution.py:32
  104.1 83.7 %reduce-scatter.5.cloned.1.call-start = ((), (), s32[]{:S(2)}) async-start(), calls=%async_computation.3 | async-start | bytes 589824 | tf_op jit(solution)/shard_map/reduce_scatter | solution.py:33
  178.6 58.5 %all-gather.4.cloned.1.call-start = ((), (), s32[]{:S(2)}) async-start(), calls=%async_computation.4 | async-start | bytes 3342336 | tf_op jit(solution)/shard_map/all_gather | solution.py:34
Sparse Core Ops, SparseCore 0:
  15.7 83.0 all-gather.5
  104.3 74.2 reduce-scatter.2
  180.8 6.8 reduce-scatter.4
  190.5 46.5 all-gather.3
